TPU v7x, 512 devices: a whole 4x8x8 slice. The times are simulated.
512 devices in a mesh: gz: 16 (over z, core), xy: 32 (over y, x).
Axes of the slice: x: 4, y: 8, z: 8, core: 2. Of those that a mesh axis runs over, the one named last changes fastest.
Arguments:
- density: float32 [512, 64, 512], P('xy', 'gz'), may hold values from 0.5 to 2
- momentum: float32 [3, 512, 64, 512], P(None, 'xy', 'gz'), may hold values from -3 to 3
- magnetic: float32 [3, 512, 64, 512], P(None, 'xy', 'gz'), may hold values from -3 to 3
- arm_potential: float32 [512, 512], P('xy'), may hold values from -10 to 10
- sn_cells: int32 [512, 3], P(('gz', 'xy')), may hold values from 0 to 511, as said below
- sn_counts: int32 [512], P(('gz', 'xy')), may hold values from 0 to 3
Outputs:
- new_density: float32 [512, 64, 512], P('xy', 'gz')
- new_momentum: float32 [3, 512, 64, 512], P(None, 'xy', 'gz')
- new_magnetic: float32 [3, 512, 64, 512], P(None, 'xy', 'gz')
- density_modes: float32 [2, 64, 512, 512], P(None, 'gz', 'xy')
Inputs may be any that keep to these rules, and one draw needn't show every extreme that they name: `sn_cells`: row e is the centre of an event held by device e // 1 of the joined axes gz+xy (gz slowest); its x lies among that device's 16 x rows and its z among its 4 z planes. `sn_counts`: 0 marks an empty slot.
All inputs are finite; a program needn't handle non-finite values.
Results may differ from a plain program's by a relative error of at most 0.00023.
Values sent between devices are 32-bit elements; how exact they have to be, the bound alone decides.
A program may use at most 128 MiB of HBM per device.

v0:
```python
import jax
import jax.numpy as jnp
import ml_dtypes
import numpy as np
from jax import lax
from jax.experimental import pallas as pl
from jax.experimental.pallas import tpu as pltpu
from jax.sharding import PartitionSpec as P

MESH = pl.DeviceIdType.MESH
F32 = jnp.float32
BF16 = jnp.bfloat16

NX, NY = 512, 512
XR, ZP = 16, 4
RX, RZ = 5, 11
SLOTS = 64
REACH = 32
A = -0.1 / 12.0
DIFF = 0.05
TILE = (XR + 4) * 8


def tables():
    wave = np.arange(NY)
    angle = (wave[:, None] * wave[None, :] % NY) * (2.0 * np.pi / NY)
    full = np.concatenate([np.cos(angle), np.sin(angle)], axis=1)
    high = full.astype(ml_dtypes.bfloat16)
    low = (full - high.astype(np.float64)).astype(ml_dtypes.bfloat16)
    return high, low


def split(value):
    high = value.astype(BF16)
    return high, (value - high.astype(F32)).astype(BF16)


def ring(flux, field, axis):
    size = flux.shape[axis]
    near = DIFF * field
    steep = (8.0 * A) * flux
    far = A * flux
    return (
        pltpu.roll(near - steep, 1, axis)
        + pltpu.roll(near + steep, size - 1, axis)
        + pltpu.roll(far, 2, axis)
        - pltpu.roll(far, size - 2, axis)
    )


def kernel(
    nxy, ngz,
    rho_ref, mom_ref, mag_ref, pot_ref, cells_ref, counts_ref, hi_ref, lo_ref,
    orho_ref, omom_ref, omag_ref, omode_ref,
    u, src, fx, pot, ev, amat, bmat, hi, lo, nd, nmom, nmag, rmat, outbox, inbox, modes,
    local_sem, evz_s, evz_r, evx_s, evx_r, halo_s, halo_r, a2a_s, a2a_r, out_sem,
):
    me_xy = lax.axis_index("xy")
    me_gz = lax.axis_index("gz")

    def xy(k):
        return lax.rem(me_xy + (k + nxy), nxy)

    def gz(k):
        return lax.rem(me_gz + (k + ngz), ngz)

    local = [
        pltpu.make_async_copy(rho_ref, u.at[0, 2:18, 2:6], local_sem.at[0]),
        pltpu.make_async_copy(mom_ref, u.at[1:4, 2:18, 2:6], local_sem.at[1]),
        pltpu.make_async_copy(mag_ref, u.at[4:7, 2:18, 2:6], local_sem.at[2]),
        pltpu.make_async_copy(pot_ref, pot.at[8:24], local_sem.at[3]),
        pltpu.make_async_copy(hi_ref, hi, local_sem.at[4]),
        pltpu.make_async_copy(lo_ref, lo, local_sem.at[5]),
    ]
    for copy in local:
        copy.start()

    lane = lax.broadcasted_iota(jnp.int32, (1, 128), 1)
    row = jnp.where(lane == 0, cells_ref[0, 0], 0)
    row = jnp.where(lane == 1, cells_ref[0, 1], row)
    row = jnp.where(lane == 2, cells_ref[0, 2], row)
    row = jnp.where(lane == 3, counts_ref[0], row)
    centre = (RX // 2) * RZ
    ev[centre + RZ // 2] = row.astype(F32)
    for slot in range(RX * RZ, SLOTS):
        ev[slot] = jnp.zeros((1, 128), F32)

    barrier = pltpu.get_barrier_semaphore()

    @pl.loop(1, nxy)
    def _(k):
        pl.semaphore_signal(barrier, inc=1, device_id={"xy": xy(k)}, device_id_type=MESH)

    zsteps = [k for k in range(-(RZ // 2), RZ // 2 + 1) if k]
    xsteps = [k for k in range(-(RX // 2), RX // 2 + 1) if k]
    for k in zsteps:
        pl.semaphore_signal(barrier, inc=1, device_id={"gz": gz(k)}, device_id_type=MESH)
    pl.semaphore_wait(barrier, nxy - 1 + len(zsteps))

    def send(source, target, sems, recvs, index, where):
        return pltpu.make_async_remote_copy(
            src_ref=source, dst_ref=target, send_sem=sems.at[index], recv_sem=recvs.at[index],
            device_id=where, device_id_type=MESH,
        )

    evz = []
    for index, k in enumerate(zsteps):
        copy = send(
            ev.at[centre + RZ // 2], ev.at[centre + RZ // 2 - k], evz_s, evz_r, index, {"gz": gz(k)}
        )
        copy.start()
        evz.append(copy)

    up, down = {"xy": xy(1)}, {"xy": xy(-1)}
    above, below = {"gz": gz(1)}, {"gz": gz(-1)}
    low_x, high_x = slice(0, 2), slice(18, 20)
    low_z, high_z = slice(0, 2), slice(6, 8)
    own_x, own_z = slice(2, 18), slice(2, 6)
    pairs = [
        (rho_ref.at[:, 2:4], u.at[0, own_x, low_z], above),
        (rho_ref.at[:, 0:2], u.at[0, own_x, high_z], below),
        (mom_ref.at[2, :, 2:4], u.at[3, own_x, low_z], above),
        (mom_ref.at[2, :, 0:2], u.at[3, own_x, high_z], below),
        (rho_ref.at[14:16], u.at[0, low_x, own_z], up),
        (rho_ref.at[0:2], u.at[0, high_x, own_z], down),
        (mom_ref.at[0, 14:16], u.at[1, low_x, own_z], up),
        (mom_ref.at[0, 0:2], u.at[1, high_x, own_z], down),
        (mom_ref.at[0:2, :, 2:4], u.at[1:3, own_x, low_z], above),
        (mom_ref.at[0:2, :, 0:2], u.at[1:3, own_x, high_z], below),
        (mag_ref.at[:, :, 2:4], u.at[4:7, own_x, low_z], above),
        (mag_ref.at[:, :, 0:2], u.at[4:7, own_x, high_z], below),
        (mom_ref.at[1:3, 14:16], u.at[2:4, low_x, own_z], up),
        (mom_ref.at[1:3, 0:2], u.at[2:4, high_x, own_z], down),
        (mag_ref.at[:, 14:16], u.at[4:7, low_x, own_z], up),
        (mag_ref.at[:, 0:2], u.at[4:7, high_x, own_z], down),
        (pot_ref.at[14:16], pot.at[6:8], up),
        (pot_ref.at[0:2], pot.at[24:26], down),
    ]
    halos = [send(s, t, halo_s, halo_r, index, w) for index, (s, t, w) in enumerate(pairs)]
    first = 8
    for copy in halos[:first]:
        copy.start()

    for copy in evz:
        copy.wait_recv()
    evx = []
    for index, k in enumerate(xsteps):
        copy = send(
            ev.at[pl.ds(centre, RZ)], ev.at[pl.ds(centre - k * RZ, RZ)], evx_s, evx_r, index,
            {"xy": xy(k)},
        )
        copy.start()
        evx.append(copy)
    for copy in halos[first:]:
        copy.start()
    for copy in evx:
        copy.wait_recv()

    events = ev[...].reshape(SLOTS, 128)
    x0 = (me_xy * XR).astype(F32)
    z0 = (me_gz * ZP).astype(F32)
    nz = float(ngz * ZP)

    def wrapped(value, period):
        value = jnp.where(value >= period / 2, value - period, value)
        return jnp.where(value < -period / 2, value + period, value)

    turned = jnp.transpose(jnp.concatenate([events, events], axis=0))
    ex = wrapped(turned[0:1] - x0, float(NX))
    ez = wrapped(turned[2:3] - z0, nz)
    cell = lax.broadcasted_iota(jnp.int32, (TILE, 128), 0)
    dx = ((cell >> 3) - 2).astype(F32) - ex
    dz = ((cell & 7) - 2).astype(F32) - ez
    room = 256.0 - dx * dx - dz * dz
    second = (lax.broadcasted_iota(jnp.int32, (1, 128), 1) >> 6).astype(F32)
    for t in range(REACH // 2):
        dy = second + float(2 * t - REACH // 2)
        amat[:, 128 * t : 128 * t + 128] = jnp.maximum(room - dy * dy, 0.0).astype(BF16)

    ey = events[:, 1:2]
    en = events[:, 3:4]
    enx = en * wrapped(events[:, 0:1] - x0, float(NX))
    enz = en * wrapped(events[:, 2:3] - z0, nz)
    column = lax.broadcasted_iota(jnp.int32, (SLOTS, NY), 1).astype(F32)

    @pl.loop(0, REACH)
    def _(step):
        dy = (step - REACH // 2).astype(F32)
        hit = ey + dy
        hit = jnp.where(hit < 0.0, hit + float(NY), hit)
        hit = jnp.where(hit >= float(NY), hit - float(NY), hit)
        match = column == hit
        rows = pl.ds(pl.multiple_of(step * SLOTS, SLOTS), SLOTS)
        for which, factor in enumerate((en, enx, en * dy, enz)):
            bmat[rows, which * NY : (which + 1) * NY] = jnp.where(match, factor, 0.0).astype(BF16)

    def total(which):
        return jnp.dot(
            amat[...], bmat[:, which * NY : (which + 1) * NY], preferred_element_type=F32
        )

    here = lax.broadcasted_iota(jnp.int32, (TILE, NY), 0)
    mass = total(0)
    block = (XR + 4, 8, NY)
    src[0] = (mass * (1.0 / 256.0)).reshape(block)
    src[1] = ((((here >> 3) - 2).astype(F32) * mass - total(1)) * (1.0 / 2048.0)).reshape(block)
    src[2] = (total(2) * (1.0 / 2048.0)).reshape(block)
    src[3] = ((((here & 7) - 2).astype(F32) * mass - total(3)) * (1.0 / 2048.0)).reshape(block)

    for copy in local:
        copy.wait()
    for copy in halos[:first]:
        copy.wait_recv()

    def with_source(field, i):
        return u[field, i] + src[field, i]

    def inner(field, i):
        return u[field, i, 2:6] + src[field, i, 2:6]

    @pl.loop(2, XR + 2)
    def _(i):
        rho = with_source(0, i)
        new = (1.0 - 6.0 * DIFF) * rho
        new += DIFF * (with_source(0, i - 1) + with_source(0, i + 1))
        new += ring(with_source(3, i), rho, 0)
        own = new[2:6] + ring(inner(2, i), rho[2:6], 1)
        own += A * (inner(1, i - 2) - inner(1, i + 2))
        own += (8.0 * A) * (inner(1, i + 1) - inner(1, i - 1))
        nd[i - 2] = own

    outs = [pltpu.make_async_copy(nd, orho_ref, out_sem.at[0])]
    outs[0].start()

    high, low = split(nd[...].reshape(XR * ZP, NY))
    both = jnp.dot(jnp.concatenate([high, low], axis=0), hi[...], preferred_element_type=F32)
    rows = XR * ZP
    full = both[:rows] + both[rows:] + jnp.dot(high, lo[...], preferred_element_type=F32)
    for t in range(2 * NY // 128):
        rmat[t] = full[:, 128 * t : 128 * t + 128]

    group = lax.broadcasted_iota(jnp.int32, (XR, 128), 1) >> 4

    @pl.loop(0, NY // 128)
    def _(t):
        parts = []
        for z in range(ZP):
            for half in range(2):
                parts.append(rmat[half * (NY // 128) + t, pl.ds(z, XR, stride=ZP), :])
        for d in range(8):
            value = parts[d]
            for g in range(8):
                if g != d:
                    value = jnp.where(group == g, pltpu.roll(parts[g], (16 * (g - d)) % 128, 1), value)
            outbox[t * 8 + d] = value

    def letter(k):
        peer = xy(k)
        return pltpu.make_async_remote_copy(
            src_ref=outbox.at[peer], dst_ref=inbox.at[me_xy], send_sem=a2a_s.at[k],
            recv_sem=a2a_r.at[k], device_id={"xy": peer}, device_id_type=MESH,
        )

    @pl.loop(1, nxy)
    def _(k):
        letter(k).start()

    inbox[me_xy] = outbox[me_xy]

    for copy in halos[first:]:
        copy.wait_recv()

    @pl.loop(0, XR + 4)
    def _(i):
        rho = with_source(0, i)
        m = [with_source(1 + c, i) for c in range(3)]
        b = [u[4 + c, i] for c in range(3)]
        u[0, i] = rho
        for c in range(3):
            u[1 + c, i] = m[c]
        inverse = 1.0 / rho
        v = [m[c] * inverse for c in range(3)]
        pressure = rho + 0.5 * (b[0] * b[0] + b[1] * b[1] + b[2] * b[2])
        fx[0, i] = m[0] * v[0] - b[0] * b[0] + pressure
        fx[1, i] = m[1] * v[0] - b[1] * b[0]
        fx[2, i] = m[2] * v[0] - b[2] * b[0]
        fx[3, i] = v[0] * b[1] - b[0] * v[1]
        fx[4, i] = v[0] * b[2] - b[0] * v[2]

    @pl.loop(2, XR + 2)
    def _(i):
        rho = u[0, i]
        m = [u[1 + c, i] for c in range(3)]
        b = [u[4 + c, i] for c in range(3)]
        inverse = 1.0 / rho
        v = [m[c] * inverse for c in range(3)]
        pressure = rho + 0.5 * (b[0] * b[0] + b[1] * b[1] + b[2] * b[2])

        def flux(c, k):
            value = m[c] * v[k] - b[c] * b[k]
            return value + pressure if c == k else value

        def along_x(field, which):
            value = DIFF * (u[field, i - 1] + u[field, i + 1])
            if which is not None:
                value += A * (fx[which, i - 2] - fx[which, i + 2])
                value += (8.0 * A) * (fx[which, i + 1] - fx[which, i - 1])
            return value

        def spread(field, axis):
            size = field.shape[axis]
            return DIFF * (pltpu.roll(field, 1, axis) + pltpu.roll(field, size - 1, axis))

        def slope(offset):
            return pot[pl.ds(i + 6 + offset, 1), :]

        keep = 1.0 - 6.0 * DIFF
        for c in range(3):
            new = keep * m[c] + along_x(1 + c, c)
            new += ring(flux(c, 1), m[c], 1)
            new += ring(flux(c, 2), m[c], 0)
            if c == 0:
                pull = A * (slope(-2) - slope(2)) + (8.0 * A) * (slope(1) - slope(-1))
                new += rho * pull
            if c == 1:
                own = jnp.broadcast_to(slope(0), (8, NY))
                pull = A * (pltpu.roll(own, 2, 1) - pltpu.roll(own, NY - 2, 1))
                pull += (8.0 * A) * (pltpu.roll(own, NY - 1, 1) - pltpu.roll(own, 1, 1))
                new += rho * pull
            nmom[c, i - 2] = new[2:6]
        for c in range(3):
            new = keep * b[c] + along_x(4 + c, None if c == 0 else 2 + c)
            if c == 1:
                new += spread(b[c], 1)
            else:
                new += ring(v[1] * b[c] - b[1] * v[c], b[c], 1)
            if c == 2:
                new += spread(b[c], 0)
            else:
                new += ring(v[2] * b[c] - b[2] * v[c], b[c], 0)
            nmag[c, i - 2] = new[2:6]

    outs.append(pltpu.make_async_copy(nmom, omom_ref, out_sem.at[1]))
    outs.append(pltpu.make_async_copy(nmag, omag_ref, out_sem.at[2]))
    outs[1].start()
    outs[2].start()

    @pl.loop(1, nxy)
    def _(k):
        pltpu.make_async_remote_copy(
            src_ref=outbox.at[me_xy], dst_ref=inbox.at[xy(-k)], send_sem=a2a_s.at[k],
            recv_sem=a2a_r.at[k], device_id={"xy": xy(k)}, device_id_type=MESH,
        ).wait_recv()

    high, low = split(inbox[...].reshape(NX, 128))

    def across(lhs, rhs):
        return lax.dot_general(
            lhs, rhs, (((0,), (0,)), ((), ())), preferred_element_type=F32
        )

    both = across(jnp.concatenate([high, low], axis=1), hi[...])
    full = both[:128] + both[128:] + across(high, lo[...])
    scale = 1.0 / 512.0
    wave_y = lax.broadcasted_iota(jnp.int32, (16, NX), 0) + me_xy * 16
    wave_x = lax.broadcasted_iota(jnp.int32, (16, NX), 1)
    origin = (wave_y == 0) & (wave_x == 0)
    for z in range(ZP):
        re = full[32 * z : 32 * z + 16]
        im = full[32 * z + 16 : 32 * z + 32]
        modes[0, z] = jnp.where(origin, 0.0, (re[:, :NX] - im[:, NX:]) * scale)
        modes[1, z] = jnp.where(origin, 0.0, (re[:, NX:] + im[:, :NX]) * -scale)
    outs.append(pltpu.make_async_copy(modes, omode_ref, out_sem.at[3]))
    outs[3].start()

    for copy in evz + evx + halos:
        copy.wait_send()

    @pl.loop(1, nxy)
    def _(k):
        letter(k).wait_send()

    for copy in outs:
        copy.wait()


def on_device(nxy, ngz, high, low, density, momentum, magnetic, arm_potential, sn_cells, sn_counts):
    hbm = pl.BlockSpec(memory_space=pl.ANY)
    smem = pl.BlockSpec(memory_space=pltpu.SMEM)
    halo = 18

    def body(*refs):
        kernel(nxy, ngz, *refs)

    dma = pltpu.SemaphoreType.DMA
    return pl.pallas_call(
        body,
        out_shape=(
            jax.ShapeDtypeStruct((XR, ZP, NY), F32),
            jax.ShapeDtypeStruct((3, XR, ZP, NY), F32),
            jax.ShapeDtypeStruct((3, XR, ZP, NY), F32),
            jax.ShapeDtypeStruct((2, ZP, 16, NX), F32),
        ),
        in_specs=[hbm, hbm, hbm, hbm, smem, smem, hbm, hbm],
        out_specs=(hbm, hbm, hbm, hbm),
        scratch_shapes=[
            pltpu.VMEM((7, XR + 4, 8, NY), F32),
            pltpu.VMEM((4, XR + 4, 8, NY), F32),
            pltpu.VMEM((5, XR + 4, 8, NY), F32),
            pltpu.VMEM((32, NY), F32),
            pltpu.VMEM((SLOTS, 1, 128), F32),
            pltpu.VMEM((TILE, REACH * SLOTS), BF16),
            pltpu.VMEM((REACH * SLOTS, 4 * NY), BF16),
            pltpu.VMEM((NY, 2 * NY), BF16),
            pltpu.VMEM((NY, 2 * NY), BF16),
            pltpu.VMEM((XR, ZP, NY), F32),
            pltpu.VMEM((3, XR, ZP, NY), F32),
            pltpu.VMEM((3, XR, ZP, NY), F32),
            pltpu.VMEM((2 * NY // 128, XR * ZP, 128), F32),
            pltpu.VMEM((nxy, XR, 128), F32),
            pltpu.VMEM((nxy, XR, 128), F32),
            pltpu.VMEM((2, ZP, 16, NX), F32),
            dma((6,)),
            dma((RZ - 1,)), dma((RZ - 1,)),
            dma((RX - 1,)), dma((RX - 1,)),
            dma((halo,)), dma((halo,)),
            dma((nxy,)), dma((nxy,)),
            dma((4,)),
        ],
        compiler_params=pltpu.CompilerParams(
            collective_id=0, has_side_effects=True
        ),
    )(density, momentum, magnetic, arm_potential, sn_cells, sn_counts, high, low)


def solution(mesh):
    nxy, ngz = mesh.shape["xy"], mesh.shape["gz"]
    high, low = tables()

    def step(*arrays):
        return on_device(nxy, ngz, jnp.asarray(high), jnp.asarray(low), *arrays)

    in_specs = (
        P("xy", "gz", None),
        P(None, "xy", "gz", None),
        P(None, "xy", "gz", None),
        P("xy", None),
        P(("gz", "xy"), None),
        P(("gz", "xy")),
    )
    out_specs = (
        P("xy", "gz", None),
        P(None, "xy", "gz", None),
        P(None, "xy", "gz", None),
        P(None, "gz", "xy", None),
    )
    return jax.shard_map(step, mesh=mesh, in_specs=in_specs, out_specs=out_specs, check_vma=False)
```

profile of v0, /device:TPU:16, one launch (start us, length us, event | category | flops | bytes accessed | tf_op | source)
XLA Modules:
  0.0 59.9 jit_solution(2339795016620806193)
XLA Ops:
  1.3 53.4 %shard_map.111 = (f32[16,4,512]{2,1,0:T(4,128)}, f32[3,16,4,512]{3,2,1,0:T(4,128)}, f32[3,16,4,512]{3,2,1,0:T(4,128)}, f32[2,4,16,512]{3,2,1,0:T(8,128)}) custom-call(f32[16,4,512]{2,1,0:T(4,128)} %refs_0_.1, f32[3,16,4,512]{3,2,1,0:T(4,128)} %refs_1_.1, f32[3,16,4,512]{3,2,1,0:T(4,128)} %refs_2_.1, f32[16,512]{1,0:T(8,128)} %refs_3_.1, s32[1,3]{1,0:T(1,128)} %refs_4_.1, ...), custom_call_target="tpu_custom_call" | custom-call | tf_op jit(solution)/shard_map/pallas_call | solution.py:396
  54.7 1.6 %copy.17 = f32[16,4,512]{2,1,0:T(4,128)} copy(f32[16,4,512]{2,1,0:T(4,128)} %get-tuple-element.8) | data formatting | bytes 262144
  56.3 0.0 copy-start
  56.3 1.8 %copy.18 = f32[3,16,4,512]{3,2,1,0:T(4,128)} copy(f32[3,16,4,512]{3,2,1,0:T(4,128)} %get-tuple-element.9) | data formatting | bytes 786432
  58.1 0.0 copy-done
  58.1 0.0 copy-start.1
  58.1 0.7 %copy.19 = f32[3,16,4,512]{3,2,1,0:T(4,128)} copy(f32[3,16,4,512]{3,2,1,0:T(4,128)S(1)} %copy-done) | data formatting | bytes 786432
  58.8 0.3 copy-done.1
  59.2 0.7 %copy.20 = f32[2,4,16,512]{3,2,1,0:T(8,128)} copy(f32[2,4,16,512]{3,2,1,0:T(8,128)S(1)} %copy-done.1) | data formatting | bytes 524288
Async XLA Ops:
  56.3 1.8 %copy-start = (f32[3,16,4,512]{3,2,1,0:T(4,128)S(1)}, f32[3,16,4,512]{3,2,1,0:T(4,128)}, u32[]{:S(2)}) copy-start(f32[3,16,4,512]{3,2,1,0:T(4,128)} %get-tuple-element.10) | copy-start | bytes 1179652
  58.1 1.1 %copy-start.1 = (f32[2,4,16,512]{3,2,1,0:T(8,128)S(1)}, f32[2,4,16,512]{3,2,1,0:T(8,128)}, u32[]{:S(2)}) copy-start(f32[2,4,16,512]{3,2,1,0:T(8,128)} %get-tuple-element.11) | copy-start | bytes 786436
where the time goes:
time: 60.1 us; the launch traced here: 59.9 us
  Pallas kernels  53.4 us (89%)
  local copies, waits for them, and re-layouts  5.18 us (9%)
  between operations  1.29 us (2%)
    pallas_call x1, Pallas kernels, on_device(): pl.pallas_call(body, out_shape=(jax.ShapeDtypeStruct((XR, ZP, NY), F32),...  53.4 us
    unnamed x8, local copies, waits for them, and re-layouts  5.18 us

commit v1 on v0

--- a/solution.py
+++ b/solution.py
@@ -15,7 +15,7 @@
 XR, ZP = 16, 4
 RX, RZ = 5, 11
 SLOTS = 64
-REACH = 32
+REACH = 16
 A = -0.1 / 12.0
 DIFF = 0.05
 TILE = (XR + 4) * 8
@@ -51,9 +51,9 @@
 def kernel(
     nxy, ngz,
     rho_ref, mom_ref, mag_ref, pot_ref, cells_ref, counts_ref, hi_ref, lo_ref,
-    orho_ref, omom_ref, omag_ref, omode_ref,
-    u, src, fx, pot, ev, amat, bmat, hi, lo, nd, nmom, nmag, rmat, outbox, inbox, modes,
-    local_sem, evz_s, evz_r, evx_s, evx_r, halo_s, halo_r, a2a_s, a2a_r, out_sem,
+    nd, nmom, nmag, modes,
+    u, src, fx, pot, ev, amat, bmat, hi, lo, rmat, outbox, inbox,
+    local_sem, ev_s, ev_r, halo_s, halo_r, a2a_s, a2a_r,
 ):
     me_xy = lax.axis_index("xy")
     me_gz = lax.axis_index("gz")
@@ -63,6 +63,24 @@
 
     def gz(k):
         return lax.rem(me_gz + (k + ngz), ngz)
+
+    barrier = pltpu.get_barrier_semaphore()
+    middle = (RX * RZ) // 2
+
+    def owner(slot):
+        return {"xy": xy(slot // RZ - RX // 2), "gz": gz(lax.rem(slot, RZ) - RZ // 2)}
+
+    def each_other_slot(body):
+        pl.loop(0, middle)(body)
+        pl.loop(middle + 1, RX * RZ)(body)
+
+    @each_other_slot
+    def _(slot):
+        pl.semaphore_signal(barrier, inc=1, device_id=owner(slot), device_id_type=MESH)
+
+    @pl.loop(RX // 2 + 1, nxy - RX // 2)
+    def _(k):
+        pl.semaphore_signal(barrier, inc=1, device_id={"xy": xy(k)}, device_id_type=MESH)
 
     local = [
         pltpu.make_async_copy(rho_ref, u.at[0, 2:18, 2:6], local_sem.at[0]),
@@ -80,22 +98,11 @@
     row = jnp.where(lane == 1, cells_ref[0, 1], row)
     row = jnp.where(lane == 2, cells_ref[0, 2], row)
     row = jnp.where(lane == 3, counts_ref[0], row)
-    centre = (RX // 2) * RZ
-    ev[centre + RZ // 2] = row.astype(F32)
+    ev[middle] = row.astype(F32)
     for slot in range(RX * RZ, SLOTS):
         ev[slot] = jnp.zeros((1, 128), F32)
 
-    barrier = pltpu.get_barrier_semaphore()
-
-    @pl.loop(1, nxy)
-    def _(k):
-        pl.semaphore_signal(barrier, inc=1, device_id={"xy": xy(k)}, device_id_type=MESH)
-
-    zsteps = [k for k in range(-(RZ // 2), RZ // 2 + 1) if k]
-    xsteps = [k for k in range(-(RX // 2), RX // 2 + 1) if k]
-    for k in zsteps:
-        pl.semaphore_signal(barrier, inc=1, device_id={"gz": gz(k)}, device_id_type=MESH)
-    pl.semaphore_wait(barrier, nxy - 1 + len(zsteps))
+    pl.semaphore_wait(barrier, RX * RZ - 1 + nxy - RX)
 
     def send(source, target, sems, recvs, index, where):
         return pltpu.make_async_remote_copy(
@@ -103,13 +110,12 @@
             device_id=where, device_id_type=MESH,
         )
 
-    evz = []
-    for index, k in enumerate(zsteps):
-        copy = send(
-            ev.at[centre + RZ // 2], ev.at[centre + RZ // 2 - k], evz_s, evz_r, index, {"gz": gz(k)}
-        )
-        copy.start()
-        evz.append(copy)
+    def event(slot):
+        return send(ev.at[middle], ev.at[slot], ev_s, ev_r, slot, owner(RX * RZ - 1 - slot))
+
+    @each_other_slot
+    def _(slot):
+        event(slot).start()
 
     up, down = {"xy": xy(1)}, {"xy": xy(-1)}
     above, below = {"gz": gz(1)}, {"gz": gz(-1)}
@@ -141,20 +147,12 @@
     for copy in halos[:first]:
         copy.start()
 
-    for copy in evz:
-        copy.wait_recv()
-    evx = []
-    for index, k in enumerate(xsteps):
-        copy = send(
-            ev.at[pl.ds(centre, RZ)], ev.at[pl.ds(centre - k * RZ, RZ)], evx_s, evx_r, index,
-            {"xy": xy(k)},
-        )
-        copy.start()
-        evx.append(copy)
     for copy in halos[first:]:
         copy.start()
-    for copy in evx:
-        copy.wait_recv()
+
+    @each_other_slot
+    def _(slot):
+        event(slot).wait_recv()
 
     events = ev[...].reshape(SLOTS, 128)
     x0 = (me_xy * XR).astype(F32)
@@ -174,25 +172,30 @@
     room = 256.0 - dx * dx - dz * dz
     second = (lax.broadcasted_iota(jnp.int32, (1, 128), 1) >> 6).astype(F32)
     for t in range(REACH // 2):
-        dy = second + float(2 * t - REACH // 2)
+        dy = second + float(2 * t)
         amat[:, 128 * t : 128 * t + 128] = jnp.maximum(room - dy * dy, 0.0).astype(BF16)
 
-    ey = events[:, 1:2]
     en = events[:, 3:4]
-    enx = en * wrapped(events[:, 0:1] - x0, float(NX))
-    enz = en * wrapped(events[:, 2:3] - z0, nz)
     column = lax.broadcasted_iota(jnp.int32, (SLOTS, NY), 1).astype(F32)
-
-    @pl.loop(0, REACH)
-    def _(step):
-        dy = (step - REACH // 2).astype(F32)
-        hit = ey + dy
-        hit = jnp.where(hit < 0.0, hit + float(NY), hit)
-        hit = jnp.where(hit >= float(NY), hit - float(NY), hit)
-        match = column == hit
-        rows = pl.ds(pl.multiple_of(step * SLOTS, SLOTS), SLOTS)
-        for which, factor in enumerate((en, enx, en * dy, enz)):
-            bmat[rows, which * NY : (which + 1) * NY] = jnp.where(match, factor, 0.0).astype(BF16)
+    away = wrapped(column - events[:, 1:2], float(NY))
+    distance = jnp.abs(away).astype(BF16)
+    def wide(value):
+        return jnp.where(column >= 0.0, value, 0.0)
+
+    number = wide(en)
+    factors = [
+        number.astype(BF16),
+        (number * wide(wrapped(events[:, 0:1] - x0, float(NX)))).astype(BF16),
+        (number * away).astype(BF16),
+        (number * wide(wrapped(events[:, 2:3] - z0, nz))).astype(BF16),
+    ]
+    nothing = jnp.zeros((SLOTS, NY), BF16)
+    for step in range(REACH):
+        match = distance == jnp.full((SLOTS, NY), step, BF16)
+        for which, factor in enumerate(factors):
+            bmat[step * SLOTS : (step + 1) * SLOTS, which * NY : (which + 1) * NY] = jnp.where(
+                match, factor, nothing
+            )
 
     def total(which):
         return jnp.dot(
@@ -228,9 +231,6 @@
         own += A * (inner(1, i - 2) - inner(1, i + 2))
         own += (8.0 * A) * (inner(1, i + 1) - inner(1, i - 1))
         nd[i - 2] = own
-
-    outs = [pltpu.make_async_copy(nd, orho_ref, out_sem.at[0])]
-    outs[0].start()
 
     high, low = split(nd[...].reshape(XR * ZP, NY))
     both = jnp.dot(jnp.concatenate([high, low], axis=0), hi[...], preferred_element_type=F32)
@@ -340,11 +340,6 @@
                 new += ring(v[2] * b[c] - b[2] * v[c], b[c], 0)
             nmag[c, i - 2] = new[2:6]
 
-    outs.append(pltpu.make_async_copy(nmom, omom_ref, out_sem.at[1]))
-    outs.append(pltpu.make_async_copy(nmag, omag_ref, out_sem.at[2]))
-    outs[1].start()
-    outs[2].start()
-
     @pl.loop(1, nxy)
     def _(k):
         pltpu.make_async_remote_copy(
@@ -370,17 +365,28 @@
         im = full[32 * z + 16 : 32 * z + 32]
         modes[0, z] = jnp.where(origin, 0.0, (re[:, :NX] - im[:, NX:]) * scale)
         modes[1, z] = jnp.where(origin, 0.0, (re[:, NX:] + im[:, :NX]) * -scale)
-    outs.append(pltpu.make_async_copy(modes, omode_ref, out_sem.at[3]))
-    outs[3].start()
-
-    for copy in evz + evx + halos:
+
+    for copy in halos:
         copy.wait_send()
+
+    @each_other_slot
+    def _(slot):
+        event(slot).wait_send()
 
     @pl.loop(1, nxy)
     def _(k):
         letter(k).wait_send()
 
-    for copy in outs:
+
+def deliver(*refs):
+    count = (len(refs) - 1) // 2
+    sems = refs[-1]
+    copies = [
+        pltpu.make_async_copy(refs[i], refs[count + i], sems.at[i]) for i in range(count)
+    ]
+    for copy in copies:
+        copy.start()
+    for copy in copies:
         copy.wait()
 
 
@@ -393,16 +399,12 @@
         kernel(nxy, ngz, *refs)
 
     dma = pltpu.SemaphoreType.DMA
-    return pl.pallas_call(
+    shapes = ((XR, ZP, NY), (3, XR, ZP, NY), (3, XR, ZP, NY), (2, ZP, 16, NX))
+    results = pl.pallas_call(
         body,
-        out_shape=(
-            jax.ShapeDtypeStruct((XR, ZP, NY), F32),
-            jax.ShapeDtypeStruct((3, XR, ZP, NY), F32),
-            jax.ShapeDtypeStruct((3, XR, ZP, NY), F32),
-            jax.ShapeDtypeStruct((2, ZP, 16, NX), F32),
-        ),
+        out_shape=tuple(pltpu.VMEM(shape, F32) for shape in shapes),
         in_specs=[hbm, hbm, hbm, hbm, smem, smem, hbm, hbm],
-        out_specs=(hbm, hbm, hbm, hbm),
+        out_specs=tuple(pl.BlockSpec(memory_space=pltpu.VMEM) for _ in shapes),
         scratch_shapes=[
             pltpu.VMEM((7, XR + 4, 8, NY), F32),
             pltpu.VMEM((4, XR + 4, 8, NY), F32),
@@ -413,24 +415,24 @@
             pltpu.VMEM((REACH * SLOTS, 4 * NY), BF16),
             pltpu.VMEM((NY, 2 * NY), BF16),
             pltpu.VMEM((NY, 2 * NY), BF16),
-            pltpu.VMEM((XR, ZP, NY), F32),
-            pltpu.VMEM((3, XR, ZP, NY), F32),
-            pltpu.VMEM((3, XR, ZP, NY), F32),
             pltpu.VMEM((2 * NY // 128, XR * ZP, 128), F32),
             pltpu.VMEM((nxy, XR, 128), F32),
             pltpu.VMEM((nxy, XR, 128), F32),
-            pltpu.VMEM((2, ZP, 16, NX), F32),
             dma((6,)),
-            dma((RZ - 1,)), dma((RZ - 1,)),
-            dma((RX - 1,)), dma((RX - 1,)),
+            dma((RX * RZ,)), dma((RX * RZ,)),
             dma((halo,)), dma((halo,)),
             dma((nxy,)), dma((nxy,)),
-            dma((4,)),
         ],
-        compiler_params=pltpu.CompilerParams(
-            collective_id=0, has_side_effects=True
-        ),
+        compiler_params=pltpu.CompilerParams(collective_id=0, has_side_effects=True),
     )(density, momentum, magnetic, arm_potential, sn_cells, sn_counts, high, low)
+    return pl.pallas_call(
+        deliver,
+        out_shape=tuple(jax.ShapeDtypeStruct(shape, F32) for shape in shapes),
+        in_specs=[hbm] * 4,
+        out_specs=(hbm,) * 4,
+        scratch_shapes=[dma((4,))],
+        compiler_params=pltpu.CompilerParams(vmem_limit_bytes=16 * 1024 * 1024),
+    )(*results)
 
 
 def solution(mesh):

time: 60.1 us -> 42.7 us (0.71)
  Pallas kernels: 53.4 us -> 41.3 us
  local copies, waits for them, and re-layouts: 5.18 us -> 0 us
    pallas_call x1 -> x2, Pallas kernels: 53.4 us -> 41.3 us  [the longest x1 40.2 us: on_device(): pl.pallas_call(body, out_shape=tuple((pltpu.VMEM(shape, F32) for shape in...]
    unnamed x8 -> x0, local copies, waits for them, and re-layouts: 5.18 us -> none
where the time goes in v1:
time: 42.7 us; the launch traced here: 42.5 us
  Pallas kernels  41.3 us (97%)
  between operations  1.29 us (3%)
    pallas_call x1, Pallas kernels, on_device(): pl.pallas_call(body, out_shape=tuple((pltpu.VMEM(shape, F32) for shape in...  40.2 us
    pallas_call x1, Pallas kernels, on_device(): pl.pallas_call(deliver, out_shape=tuple((jax.ShapeDtypeStruct(shape, F32)...  1.04 us

profile of v1, /device:TPU:16, one launch (start us, length us, event | category | flops | bytes accessed | tf_op | source)
XLA Modules:
  0.0 42.5 jit_solution(11456922456630266679)
XLA Ops:
  1.3 40.2 %shard_map.111 = (f32[16,4,512]{2,1,0:T(4,128)S(1)}, f32[3,16,4,512]{3,2,1,0:T(4,128)S(1)}, f32[3,16,4,512]{3,2,1,0:T(4,128)S(1)}, f32[2,4,16,512]{3,2,1,0:T(8,128)S(1)}) custom-call(f32[16,4,512]{2,1,0:T(4,128)} %refs_0_.1, f32[3,16,4,512]{3,2,1,0:T(4,128)} %refs_1_.1, f32[3,16,4,512]{3,2,1,0:T(4,128)} %refs_2_.1, f32[16,512]{1,0:T(8,128)} %refs_3_.1, ...), custom_call_target="tpu_custom_call" | custom-call | tf_op jit(solution)/shard_map/pallas_call | solution.py:403
  41.5 1.0 %shard_map.112 = (f32[16,4,512]{2,1,0:T(4,128)}, f32[3,16,4,512]{3,2,1,0:T(4,128)}, f32[3,16,4,512]{3,2,1,0:T(4,128)}, f32[2,4,16,512]{3,2,1,0:T(8,128)}) custom-call(f32[16,4,512]{2,1,0:T(4,128)S(1)} %get-tuple-element.8.refs_0_, f32[3,16,4,512]{3,2,1,0:T(4,128)S(1)} %get-tuple-element.9.refs_1_, f32[3,16,4,512]{3,2,1,0:T(4,128)S(1)} %get-tuple-element.10.refs_2_, ...), custom_call_target="tpu_custom_call" | custom-call | tf_op jit(solution)/shard_map/pallas_call | solution.py:428

commit v2 on v1

--- a/solution.py
+++ b/solution.py
@@ -58,29 +58,28 @@
     me_xy = lax.axis_index("xy")
     me_gz = lax.axis_index("gz")
 
-    def xy(k):
-        return lax.rem(me_xy + (k + nxy), nxy)
-
-    def gz(k):
-        return lax.rem(me_gz + (k + ngz), ngz)
+    def shifted(me, k, size):
+        there = me + k
+        if k < 0:
+            return jnp.where(there < 0, there + size, there)
+        return jnp.where(there >= size, there - size, there)
+
+    row_of = {k: shifted(me_xy, k, nxy) for k in range(-(nxy // 2), nxy - nxy // 2)}
+    plane_of = {k: shifted(me_gz, k, ngz) for k in range(-(RZ // 2), RZ // 2 + 1)}
+    peers = sorted((k for k in row_of if k), key=lambda k: (-abs(k), k))
 
     barrier = pltpu.get_barrier_semaphore()
     middle = (RX * RZ) // 2
+    slots = [slot for slot in range(RX * RZ) if slot != middle]
 
     def owner(slot):
-        return {"xy": xy(slot // RZ - RX // 2), "gz": gz(lax.rem(slot, RZ) - RZ // 2)}
-
-    def each_other_slot(body):
-        pl.loop(0, middle)(body)
-        pl.loop(middle + 1, RX * RZ)(body)
-
-    @each_other_slot
-    def _(slot):
+        return {"xy": row_of[slot // RZ - RX // 2], "gz": plane_of[slot % RZ - RZ // 2]}
+
+    beyond = [k for k in peers if abs(k) > RX // 2]
+    for slot in slots:
         pl.semaphore_signal(barrier, inc=1, device_id=owner(slot), device_id_type=MESH)
-
-    @pl.loop(RX // 2 + 1, nxy - RX // 2)
-    def _(k):
-        pl.semaphore_signal(barrier, inc=1, device_id={"xy": xy(k)}, device_id_type=MESH)
+    for k in beyond:
+        pl.semaphore_signal(barrier, inc=1, device_id={"xy": row_of[k]}, device_id_type=MESH)
 
     local = [
         pltpu.make_async_copy(rho_ref, u.at[0, 2:18, 2:6], local_sem.at[0]),
@@ -102,7 +101,7 @@
     for slot in range(RX * RZ, SLOTS):
         ev[slot] = jnp.zeros((1, 128), F32)
 
-    pl.semaphore_wait(barrier, RX * RZ - 1 + nxy - RX)
+    pl.semaphore_wait(barrier, len(slots) + len(beyond))
 
     def send(source, target, sems, recvs, index, where):
         return pltpu.make_async_remote_copy(
@@ -113,12 +112,11 @@
     def event(slot):
         return send(ev.at[middle], ev.at[slot], ev_s, ev_r, slot, owner(RX * RZ - 1 - slot))
 
-    @each_other_slot
-    def _(slot):
+    for slot in slots:
         event(slot).start()
 
-    up, down = {"xy": xy(1)}, {"xy": xy(-1)}
-    above, below = {"gz": gz(1)}, {"gz": gz(-1)}
+    up, down = {"xy": row_of[1]}, {"xy": row_of[-1]}
+    above, below = {"gz": plane_of[1]}, {"gz": plane_of[-1]}
     low_x, high_x = slice(0, 2), slice(18, 20)
     low_z, high_z = slice(0, 2), slice(6, 8)
     own_x, own_z = slice(2, 18), slice(2, 6)
@@ -150,8 +148,7 @@
     for copy in halos[first:]:
         copy.start()
 
-    @each_other_slot
-    def _(slot):
+    for slot in slots:
         event(slot).wait_recv()
 
     events = ev[...].reshape(SLOTS, 128)
@@ -255,15 +252,14 @@
             outbox[t * 8 + d] = value
 
     def letter(k):
-        peer = xy(k)
         return pltpu.make_async_remote_copy(
-            src_ref=outbox.at[peer], dst_ref=inbox.at[me_xy], send_sem=a2a_s.at[k],
-            recv_sem=a2a_r.at[k], device_id={"xy": peer}, device_id_type=MESH,
+            src_ref=outbox.at[row_of[k]], dst_ref=inbox.at[me_xy], send_sem=a2a_s.at[k % nxy],
+            recv_sem=a2a_r.at[k % nxy], device_id={"xy": row_of[k]}, device_id_type=MESH,
         )
 
-    @pl.loop(1, nxy)
-    def _(k):
-        letter(k).start()
+    letters = [letter(k) for k in peers]
+    for copy in letters:
+        copy.start()
 
     inbox[me_xy] = outbox[me_xy]
 
@@ -340,12 +336,8 @@
                 new += ring(v[2] * b[c] - b[2] * v[c], b[c], 0)
             nmag[c, i - 2] = new[2:6]
 
-    @pl.loop(1, nxy)
-    def _(k):
-        pltpu.make_async_remote_copy(
-            src_ref=outbox.at[me_xy], dst_ref=inbox.at[xy(-k)], send_sem=a2a_s.at[k],
-            recv_sem=a2a_r.at[k], device_id={"xy": xy(k)}, device_id_type=MESH,
-        ).wait_recv()
+    for copy in letters:
+        copy.wait_recv()
 
     high, low = split(inbox[...].reshape(NX, 128))
 
@@ -369,13 +361,11 @@
     for copy in halos:
         copy.wait_send()
 
-    @each_other_slot
-    def _(slot):
+    for slot in slots:
         event(slot).wait_send()
 
-    @pl.loop(1, nxy)
-    def _(k):
-        letter(k).wait_send()
+    for copy in letters:
+        copy.wait_send()
 
 
 def deliver(*refs):

time: 42.7 us -> 41.2 us (0.965)
  the two profiles are of different devices: /device:TPU:16 before, /device:TPU:1 now
where the time goes in v2:
time: 41.2 us; the launch traced here: 41.1 us
  Pallas kernels  39.8 us (97%)
  between operations  1.29 us (3%)
    pallas_call x1, Pallas kernels, on_device(): pl.pallas_call(body, out_shape=tuple((pltpu.VMEM(shape, F32) for shape in...  38.7 us
    pallas_call x1, Pallas kernels, on_device(): pl.pallas_call(deliver, out_shape=tuple((jax.ShapeDtypeStruct(shape, F32)...  1.04 us

profile of v2, /device:TPU:1, one launch (start us, length us, event | category | flops | bytes accessed | tf_op | source)
XLA Modules:
  0.0 41.1 jit_solution(16089182075315174030)
XLA Ops:
  1.3 38.7 %shard_map.111 = (f32[16,4,512]{2,1,0:T(4,128)S(1)}, f32[3,16,4,512]{3,2,1,0:T(4,128)S(1)}, f32[3,16,4,512]{3,2,1,0:T(4,128)S(1)}, f32[2,4,16,512]{3,2,1,0:T(8,128)S(1)}) custom-call(f32[16,4,512]{2,1,0:T(4,128)} %refs_0_.1, f32[3,16,4,512]{3,2,1,0:T(4,128)} %refs_1_.1, f32[3,16,4,512]{3,2,1,0:T(4,128)} %refs_2_.1, f32[16,512]{1,0:T(8,128)} %refs_3_.1, ...), custom_call_target="tpu_custom_call" | custom-call | tf_op jit(solution)/shard_map/pallas_call | solution.py:393
  40.0 1.0 %shard_map.112 = (f32[16,4,512]{2,1,0:T(4,128)}, f32[3,16,4,512]{3,2,1,0:T(4,128)}, f32[3,16,4,512]{3,2,1,0:T(4,128)}, f32[2,4,16,512]{3,2,1,0:T(8,128)}) custom-call(f32[16,4,512]{2,1,0:T(4,128)S(1)} %get-tuple-element.8.refs_0_, f32[3,16,4,512]{3,2,1,0:T(4,128)S(1)} %get-tuple-element.9.refs_1_, f32[3,16,4,512]{3,2,1,0:T(4,128)S(1)} %get-tuple-element.10.refs_2_, ...), custom_call_target="tpu_custom_call" | custom-call | tf_op jit(solution)/shard_map/pallas_call | solution.py:418

commit v3 on v2

--- a/solution.py
+++ b/solution.py
@@ -16,6 +16,7 @@
 RX, RZ = 5, 11
 SLOTS = 64
 REACH = 16
+TORUS_X = 4
 A = -0.1 / 12.0
 DIFF = 0.05
 TILE = (XR + 4) * 8
@@ -68,6 +69,17 @@
     plane_of = {k: shifted(me_gz, k, ngz) for k in range(-(RZ // 2), RZ // 2 + 1)}
     peers = sorted((k for k in row_of if k), key=lambda k: (-abs(k), k))
 
+    ny = nxy // TORUS_X
+    me_y = me_xy // TORUS_X
+    me_x = me_xy - TORUS_X * me_y
+    y_order = [ny // 2] + [sign * k for k in range(ny // 2 - 1, 0, -1) for sign in (-1, 1)] + [0]
+    peer_ids = [
+        shifted(me_y, dy, ny) * TORUS_X + shifted(me_x, dx, TORUS_X)
+        for dx in (2, 1, 3, 0)
+        for dy in y_order
+        if dx or dy
+    ]
+
     barrier = pltpu.get_barrier_semaphore()
     middle = (RX * RZ) // 2
     slots = [slot for slot in range(RX * RZ) if slot != middle]
@@ -109,8 +121,11 @@
             device_id=where, device_id_type=MESH,
         )
 
+    def drain(sem, ref):
+        pltpu.make_async_copy(ref, ref, sem).wait()
+
     def event(slot):
-        return send(ev.at[middle], ev.at[slot], ev_s, ev_r, slot, owner(RX * RZ - 1 - slot))
+        return send(ev.at[middle], ev.at[slot], ev_s, ev_r, 0, owner(RX * RZ - 1 - slot))
 
     for slot in slots:
         event(slot).start()
@@ -148,8 +163,7 @@
     for copy in halos[first:]:
         copy.start()
 
-    for slot in slots:
-        event(slot).wait_recv()
+    drain(ev_r.at[0], ev.at[0 : len(slots)])
 
     events = ev[...].reshape(SLOTS, 128)
     x0 = (me_xy * XR).astype(F32)
@@ -251,15 +265,8 @@
                     value = jnp.where(group == g, pltpu.roll(parts[g], (16 * (g - d)) % 128, 1), value)
             outbox[t * 8 + d] = value
 
-    def letter(k):
-        return pltpu.make_async_remote_copy(
-            src_ref=outbox.at[row_of[k]], dst_ref=inbox.at[me_xy], send_sem=a2a_s.at[k % nxy],
-            recv_sem=a2a_r.at[k % nxy], device_id={"xy": row_of[k]}, device_id_type=MESH,
-        )
-
-    letters = [letter(k) for k in peers]
-    for copy in letters:
-        copy.start()
+    for peer in peer_ids:
+        send(outbox.at[peer], inbox.at[me_xy], a2a_s, a2a_r, 0, {"xy": peer}).start()
 
     inbox[me_xy] = outbox[me_xy]
 
@@ -336,8 +343,11 @@
                 new += ring(v[2] * b[c] - b[2] * v[c], b[c], 0)
             nmag[c, i - 2] = new[2:6]
 
-    for copy in letters:
-        copy.wait_recv()
+    for copy in halos:
+        copy.wait_send()
+    drain(ev_s.at[0], ev.at[0 : len(slots)])
+    drain(a2a_s.at[0], outbox.at[0 : nxy - 1])
+    drain(a2a_r.at[0], inbox.at[0 : nxy - 1])
 
     high, low = split(inbox[...].reshape(NX, 128))
 
@@ -357,15 +367,6 @@
         im = full[32 * z + 16 : 32 * z + 32]
         modes[0, z] = jnp.where(origin, 0.0, (re[:, :NX] - im[:, NX:]) * scale)
         modes[1, z] = jnp.where(origin, 0.0, (re[:, NX:] + im[:, :NX]) * -scale)
-
-    for copy in halos:
-        copy.wait_send()
-
-    for slot in slots:
-        event(slot).wait_send()
-
-    for copy in letters:
-        copy.wait_send()
 
 
 def deliver(*refs):
@@ -409,9 +410,9 @@
             pltpu.VMEM((nxy, XR, 128), F32),
             pltpu.VMEM((nxy, XR, 128), F32),
             dma((6,)),
-            dma((RX * RZ,)), dma((RX * RZ,)),
+            dma((1,)), dma((1,)),
             dma((halo,)), dma((halo,)),
-            dma((nxy,)), dma((nxy,)),
+            dma((1,)), dma((1,)),
         ],
         compiler_params=pltpu.CompilerParams(collective_id=0, has_side_effects=True),
     )(density, momentum, magnetic, arm_potential, sn_cells, sn_counts, high, low)

time: 41.2 us -> 38.7 us (0.939)
  Pallas kernels: 39.8 us -> 37.3 us
    pallas_call x1, Pallas kernels: 38.7 us -> 36.2 us  [on_device(): pl.pallas_call(body, out_shape=tuple((pltpu.VMEM(shape, F32) for shape in...]
where the time goes in v3:
time: 38.7 us; the launch traced here: 38.6 us
  Pallas kernels  37.3 us (96%)
  between operations  1.29 us (3%)
    pallas_call x1, Pallas kernels, on_device(): pl.pallas_call(body, out_shape=tuple((pltpu.VMEM(shape, F32) for shape in...  36.2 us
    pallas_call x1, Pallas kernels, on_device(): pl.pallas_call(deliver, out_shape=tuple((jax.ShapeDtypeStruct(shape, F32)...  1.04 us

profile of v3, /device:TPU:1, one launch (start us, length us, event | category | flops | bytes accessed | tf_op | source)
XLA Modules:
  0.0 38.6 jit_solution(16055834987007657595)
XLA Ops:
  1.3 36.2 %shard_map.111 = (f32[16,4,512]{2,1,0:T(4,128)S(1)}, f32[3,16,4,512]{3,2,1,0:T(4,128)S(1)}, f32[3,16,4,512]{3,2,1,0:T(4,128)S(1)}, f32[2,4,16,512]{3,2,1,0:T(8,128)S(1)}) custom-call(f32[16,4,512]{2,1,0:T(4,128)} %refs_0_.1, f32[3,16,4,512]{3,2,1,0:T(4,128)} %refs_1_.1, f32[3,16,4,512]{3,2,1,0:T(4,128)} %refs_2_.1, f32[16,512]{1,0:T(8,128)} %refs_3_.1, ...), custom_call_target="tpu_custom_call" | custom-call | tf_op jit(solution)/shard_map/pallas_call | solution.py:394
  37.5 1.0 %shard_map.112 = (f32[16,4,512]{2,1,0:T(4,128)}, f32[3,16,4,512]{3,2,1,0:T(4,128)}, f32[3,16,4,512]{3,2,1,0:T(4,128)}, f32[2,4,16,512]{3,2,1,0:T(8,128)}) custom-call(f32[16,4,512]{2,1,0:T(4,128)S(1)} %get-tuple-element.8.refs_0_, f32[3,16,4,512]{3,2,1,0:T(4,128)S(1)} %get-tuple-element.9.refs_1_, f32[3,16,4,512]{3,2,1,0:T(4,128)S(1)} %get-tuple-element.10.refs_2_, ...), custom_call_target="tpu_custom_call" | custom-call | tf_op jit(solution)/shard_map/pallas_call | solution.py:419

commit v4 on v3

--- a/solution.py
+++ b/solution.py
@@ -53,7 +53,7 @@
     nxy, ngz,
     rho_ref, mom_ref, mag_ref, pot_ref, cells_ref, counts_ref, hi_ref, lo_ref,
     nd, nmom, nmag, modes,
-    u, src, fx, pot, ev, amat, bmat, hi, lo, rmat, outbox, inbox,
+    u, src, fx, pot, ev, amat, bmat, hi, lo, rmat, outbox, inbox, cells, counts,
     local_sem, ev_s, ev_r, halo_s, halo_r, a2a_s, a2a_r,
 ):
     me_xy = lax.axis_index("xy")
@@ -80,6 +80,13 @@
         if dx or dy
     ]
 
+    fetch = [
+        pltpu.make_async_copy(cells_ref, cells, local_sem.at[6]),
+        pltpu.make_async_copy(counts_ref, counts, local_sem.at[7]),
+    ]
+    for copy in fetch:
+        copy.start()
+
     barrier = pltpu.get_barrier_semaphore()
     middle = (RX * RZ) // 2
     slots = [slot for slot in range(RX * RZ) if slot != middle]
@@ -104,11 +111,13 @@
     for copy in local:
         copy.start()
 
+    for copy in fetch:
+        copy.wait()
     lane = lax.broadcasted_iota(jnp.int32, (1, 128), 1)
-    row = jnp.where(lane == 0, cells_ref[0, 0], 0)
-    row = jnp.where(lane == 1, cells_ref[0, 1], row)
-    row = jnp.where(lane == 2, cells_ref[0, 2], row)
-    row = jnp.where(lane == 3, counts_ref[0], row)
+    row = jnp.where(lane == 0, cells[0, 0], 0)
+    row = jnp.where(lane == 1, cells[0, 1], row)
+    row = jnp.where(lane == 2, cells[0, 2], row)
+    row = jnp.where(lane == 3, counts[0], row)
     ev[middle] = row.astype(F32)
     for slot in range(RX * RZ, SLOTS):
         ev[slot] = jnp.zeros((1, 128), F32)
@@ -383,7 +392,6 @@
 
 def on_device(nxy, ngz, high, low, density, momentum, magnetic, arm_potential, sn_cells, sn_counts):
     hbm = pl.BlockSpec(memory_space=pl.ANY)
-    smem = pl.BlockSpec(memory_space=pltpu.SMEM)
     halo = 18
 
     def body(*refs):
@@ -394,7 +402,7 @@
     results = pl.pallas_call(
         body,
         out_shape=tuple(pltpu.VMEM(shape, F32) for shape in shapes),
-        in_specs=[hbm, hbm, hbm, hbm, smem, smem, hbm, hbm],
+        in_specs=[hbm] * 8,
         out_specs=tuple(pl.BlockSpec(memory_space=pltpu.VMEM) for _ in shapes),
         scratch_shapes=[
             pltpu.VMEM((7, XR + 4, 8, NY), F32),
@@ -409,7 +417,9 @@
             pltpu.VMEM((2 * NY // 128, XR * ZP, 128), F32),
             pltpu.VMEM((nxy, XR, 128), F32),
             pltpu.VMEM((nxy, XR, 128), F32),
-            dma((6,)),
+            pltpu.SMEM((1, 3), jnp.int32),
+            pltpu.SMEM((1,), jnp.int32),
+            dma((8,)),
             dma((1,)), dma((1,)),
             dma((halo,)), dma((halo,)),
             dma((1,)), dma((1,)),

time: 38.7 us -> 38.2 us (0.987)
  Pallas kernels: 37.3 us -> 36.8 us
    pallas_call x1, Pallas kernels: 36.2 us -> 35.7 us  [on_device(): pl.pallas_call(body, out_shape=tuple((pltpu.VMEM(shape, F32) for shape in...]
where the time goes in v4:
time: 38.2 us; the launch traced here: 38 us
  Pallas kernels  36.8 us (96%)
  between operations  1.29 us (3%)
    pallas_call x1, Pallas kernels, on_device(): pl.pallas_call(body, out_shape=tuple((pltpu.VMEM(shape, F32) for shape in...  35.7 us
    pallas_call x1, Pallas kernels, on_device(): pl.pallas_call(deliver, out_shape=tuple((jax.ShapeDtypeStruct(shape, F32)...  1.04 us

profile of v4, /device:TPU:1, one launch (start us, length us, event | category | flops | bytes accessed | tf_op | source)
XLA Modules:
  0.0 38.0 jit_solution(16808826375028157170)
XLA Ops:
  1.3 35.7 %shard_map.111 = (f32[16,4,512]{2,1,0:T(4,128)S(1)}, f32[3,16,4,512]{3,2,1,0:T(4,128)S(1)}, f32[3,16,4,512]{3,2,1,0:T(4,128)S(1)}, f32[2,4,16,512]{3,2,1,0:T(8,128)S(1)}) custom-call(f32[16,4,512]{2,1,0:T(4,128)} %refs_0_.1, f32[3,16,4,512]{3,2,1,0:T(4,128)} %refs_1_.1, f32[3,16,4,512]{3,2,1,0:T(4,128)} %refs_2_.1, f32[16,512]{1,0:T(8,128)} %refs_3_.1, ...), custom_call_target="tpu_custom_call" | custom-call | tf_op jit(solution)/shard_map/pallas_call | solution.py:402
  37.0 1.0 %shard_map.112 = (f32[16,4,512]{2,1,0:T(4,128)}, f32[3,16,4,512]{3,2,1,0:T(4,128)}, f32[3,16,4,512]{3,2,1,0:T(4,128)}, f32[2,4,16,512]{3,2,1,0:T(8,128)}) custom-call(f32[16,4,512]{2,1,0:T(4,128)S(1)} %get-tuple-element.8.refs_0_, f32[3,16,4,512]{3,2,1,0:T(4,128)S(1)} %get-tuple-element.9.refs_1_, f32[3,16,4,512]{3,2,1,0:T(4,128)S(1)} %get-tuple-element.10.refs_2_, ...), custom_call_target="tpu_custom_call" | custom-call | tf_op jit(solution)/shard_map/pallas_call | solution.py:429

commit v5 on v4

--- a/solution.py
+++ b/solution.py
@@ -1,3 +1,5 @@
+import functools
+
 import jax
 import jax.numpy as jnp
 import ml_dtypes
@@ -16,7 +18,6 @@
 RX, RZ = 5, 11
 SLOTS = 64
 REACH = 16
-TORUS_X = 4
 A = -0.1 / 12.0
 DIFF = 0.05
 TILE = (XR + 4) * 8
@@ -68,17 +69,6 @@
     row_of = {k: shifted(me_xy, k, nxy) for k in range(-(nxy // 2), nxy - nxy // 2)}
     plane_of = {k: shifted(me_gz, k, ngz) for k in range(-(RZ // 2), RZ // 2 + 1)}
     peers = sorted((k for k in row_of if k), key=lambda k: (-abs(k), k))
-
-    ny = nxy // TORUS_X
-    me_y = me_xy // TORUS_X
-    me_x = me_xy - TORUS_X * me_y
-    y_order = [ny // 2] + [sign * k for k in range(ny // 2 - 1, 0, -1) for sign in (-1, 1)] + [0]
-    peer_ids = [
-        shifted(me_y, dy, ny) * TORUS_X + shifted(me_x, dx, TORUS_X)
-        for dx in (2, 1, 3, 0)
-        for dy in y_order
-        if dx or dy
-    ]
 
     fetch = [
         pltpu.make_async_copy(cells_ref, cells, local_sem.at[6]),
@@ -261,8 +251,7 @@
 
     group = lax.broadcasted_iota(jnp.int32, (XR, 128), 1) >> 4
 
-    @pl.loop(0, NY // 128)
-    def _(t):
+    def sort(t):
         parts = []
         for z in range(ZP):
             for half in range(2):
@@ -274,8 +263,20 @@
                     value = jnp.where(group == g, pltpu.roll(parts[g], (16 * (g - d)) % 128, 1), value)
             outbox[t * 8 + d] = value
 
-    for peer in peer_ids:
+    def post(peer):
         send(outbox.at[peer], inbox.at[me_xy], a2a_s, a2a_r, 0, {"xy": peer}).start()
+
+    eights = nxy // 8
+    my_eight = me_xy // 8
+    for away_by in [3, 1, 2, 0]:
+        t = shifted(my_eight, away_by, eights)
+        sort(t)
+        for d in range(8):
+            peer = t * 8 + d
+            if away_by:
+                post(peer)
+            else:
+                pl.when(peer != me_xy)(functools.partial(post, peer))
 
     inbox[me_xy] = outbox[me_xy]
 

time: 38.2 us -> 37.6 us (0.984)
  the two profiles are of different devices: /device:TPU:1 before, /device:TPU:6 now
where the time goes in v5:
time: 37.6 us; the launch traced here: 37.5 us
  Pallas kernels  36.2 us (96%)
  between operations  1.29 us (3%)
    pallas_call x1, Pallas kernels, on_device(): pl.pallas_call(body, out_shape=tuple((pltpu.VMEM(shape, F32) for shape in...  35.2 us
    pallas_call x1, Pallas kernels, on_device(): pl.pallas_call(deliver, out_shape=tuple((jax.ShapeDtypeStruct(shape, F32)...  1.04 us

profile of v5, /device:TPU:6, one launch (start us, length us, event | category | flops | bytes accessed | tf_op | source)
XLA Modules:
  0.0 37.5 jit_solution(9539048870083787617)
XLA Ops:
  1.3 35.2 %shard_map.111 = (f32[16,4,512]{2,1,0:T(4,128)S(1)}, f32[3,16,4,512]{3,2,1,0:T(4,128)S(1)}, f32[3,16,4,512]{3,2,1,0:T(4,128)S(1)}, f32[2,4,16,512]{3,2,1,0:T(8,128)S(1)}) custom-call(f32[16,4,512]{2,1,0:T(4,128)} %refs_0_.1, f32[3,16,4,512]{3,2,1,0:T(4,128)} %refs_1_.1, f32[3,16,4,512]{3,2,1,0:T(4,128)} %refs_2_.1, f32[16,512]{1,0:T(8,128)} %refs_3_.1, ...), custom_call_target="tpu_custom_call" | custom-call | tf_op jit(solution)/shard_map/pallas_call | solution.py:403
  36.4 1.0 %shard_map.112 = (f32[16,4,512]{2,1,0:T(4,128)}, f32[3,16,4,512]{3,2,1,0:T(4,128)}, f32[3,16,4,512]{3,2,1,0:T(4,128)}, f32[2,4,16,512]{3,2,1,0:T(8,128)}) custom-call(f32[16,4,512]{2,1,0:T(4,128)S(1)} %get-tuple-element.8.refs_0_, f32[3,16,4,512]{3,2,1,0:T(4,128)S(1)} %get-tuple-element.9.refs_1_, f32[3,16,4,512]{3,2,1,0:T(4,128)S(1)} %get-tuple-element.10.refs_2_, ...), custom_call_target="tpu_custom_call" | custom-call | tf_op jit(solution)/shard_map/pallas_call | solution.py:430
